TPU v7x, 256 devices: a whole 4x4x8 slice. The times are simulated.
256 devices in a mesh: tm: 4 (over x), rows: 64 (over y, z, core).
Axes of the slice: x: 4, y: 4, z: 8, core: 2. Of those that a mesh axis runs over, the one named last changes fastest.
Arguments:
- latent: bfloat16 [4, 64, 160, 512], P('tm', 'rows'), may hold values from -350 to 350, as said below
- norm_gain: float32 [512], replicated, may hold values from 0.1 to 1.9
- norm_bias: float32 [512], replicated, may hold values from -4 to 4
- conv_weight: bfloat16 [3, 3, 3, 512, 512], P(None, None, None, 'rows', 'tm'), may hold values from -0.0546875 to 0.0546875
- cotangent: bfloat16 [4, 128, 320, 512], P('tm', 'rows'), may hold values from -180 to 180
Outputs:
- latent_grad: float32 [4, 64, 160, 512], P('tm', 'rows')
- gain_grad: float32 [512], replicated
- bias_grad: float32 [512], replicated
Inputs may be any that keep to these rules, and one draw needn't show every extreme that they name: `latent`: features of the unit's input.
All inputs are finite; a program needn't handle non-finite values.
Results may differ from a plain program's by a relative error of at most 0.0003.
Values may be sent and summed in bfloat16 or wider, within the bound.
No kernel may reach another device: no remote copies, remote signals or barrier semaphores. Data moves between devices by JAX's collectives and lax.ppermute only.
A program may use at most 320 MiB of HBM per device.

v0:
```python
import jax
import jax.numpy as jnp
from jax import lax
from jax.sharding import PartitionSpec as P

GROUPS = 32


def extended(block, sides, width):
    for axis, dim in sides:
        count = lax.axis_size(axis)
        forward = [(i, i + 1) for i in range(count - 1)]
        backward = [(target, source) for source, target in forward]
        low = lax.ppermute(
            lax.slice_in_dim(block, block.shape[dim] - width, None, axis=dim), axis, forward
        )
        high = lax.ppermute(lax.slice_in_dim(block, 0, width, axis=dim), axis, backward)
        block = jnp.concatenate([low, block, high], axis=dim)
    return block


def from_behind(value, axis, steps):
    count = lax.axis_size(axis)
    first, last = (max(0, -steps), min(count, count - steps))
    return lax.ppermute(value, axis, [(source, source + steps) for source in range(first, last)])


def shifted_rows(frames, extra_frames):
    padded = jnp.pad(frames, ((0, extra_frames), (0, 0), (1, 1), (0, 0)))
    fine_rows = frames.shape[1] - 2
    return [padded[:, 2 - row_tap : 2 - row_tap + fine_rows] for row_tap in range(3)]


def tap_total(row_slabs, weights, tap_pairs, frames_out, span_cols):
    running = None
    for offset, tap_index in tap_pairs:
        for row_tap in range(3):
            source = row_slabs[row_tap][offset : offset + frames_out]
            for col_tap in range(3):
                product = lax.dot_general(
                    source,
                    weights[tap_index, row_tap, col_tap],
                    (((3,), (1,)), ((), ())),
                    preferred_element_type=jnp.float32,
                )
                piece = product[:, :, 2 - col_tap : 2 - col_tap + span_cols, :]
                running = piece if running is None else running + piece
    return running


def pool_pairs(fine_grad):
    frames, fine_rows, span_cols, channels = fine_grad.shape
    return fine_grad.reshape(frames, fine_rows // 2, 2, span_cols // 2, 2, channels).sum(
        axis=(2, 4)
    )


def block_grad(row_slabs, weights, frames_out, first_frame):
    span_cols = row_slabs[0].shape[2] - 2

    def extra_terms():
        return tap_total(row_slabs, weights, ((0, 1), (0, 0), (1, 0)), 1, span_cols)

    def no_terms():
        return jnp.zeros((1, row_slabs[0].shape[1], span_cols, weights.shape[3]), jnp.float32)

    main_part = tap_total(row_slabs, weights, ((0, 2), (1, 1), (2, 0)), frames_out, span_cols)
    main_part = main_part + lax.cond(first_frame, extra_terms, no_terms)
    return pool_pairs(main_part)


def on_device(latent, norm_gain, norm_bias, conv_weight, cotangent):
    frames_all = lax.axis_size("tm")
    rows_all = lax.axis_size("rows")
    low_rows = latent.shape[1]
    low_cols = latent.shape[2]
    channels = latent.shape[3]
    per_group = channels // GROUPS
    cell_count = frames_all * rows_all * low_rows * low_cols
    rimmed = extended(cotangent, (("rows", 1),), 1)
    following = from_behind(rimmed, "tm", -1)
    further = from_behind(rimmed, "tm", -2)
    stacked = jnp.concatenate([rimmed, following, further], axis=0)
    weight_wide = lax.all_gather(conv_weight, "tm", axis=4, tiled=True)
    weight_full = lax.all_gather(weight_wide, "rows", axis=3, tiled=True)
    up_grad = block_grad(shifted_rows(stacked, 0), weight_full, 1, lax.axis_index("tm") == 0)
    features = latent.astype(jnp.float32)
    sum_x = jnp.sum(features, axis=(0, 1, 2))
    sum_sq = jnp.sum(features * features, axis=(0, 1, 2))
    total_x, total_sq = lax.psum((sum_x, sum_sq), ("tm", "rows"))
    group_x = total_x.reshape(GROUPS, per_group).sum(axis=1)
    group_sq = total_sq.reshape(GROUPS, per_group).sum(axis=1)
    group_mean = group_x / (cell_count * per_group)
    group_var = group_sq / (cell_count * per_group) - group_mean * group_mean
    inv_std = lax.rsqrt(group_var + 1e-06)
    mean_chan = jnp.repeat(group_mean, per_group)
    inv_chan = jnp.repeat(inv_std, per_group)
    normed = (features - mean_chan) * inv_chan
    pre = normed * norm_gain + norm_bias
    sigmoid_pre = jax.nn.sigmoid(pre)
    act_grad = up_grad * sigmoid_pre * (1.0 + pre * (1.0 - sigmoid_pre))
    sum_act, sum_scaled = lax.psum(
        (jnp.sum(act_grad, axis=(0, 1, 2)), jnp.sum(act_grad * normed, axis=(0, 1, 2))),
        ("tm", "rows"),
    )
    gain_grad = sum_scaled / cell_count
    bias_grad = sum_act / cell_count
    mean_q = (norm_gain * sum_act).reshape(GROUPS, per_group).sum(axis=1) / (cell_count * per_group)
    mean_qn = (norm_gain * sum_scaled).reshape(GROUPS, per_group).sum(axis=1) / (
        cell_count * per_group
    )
    latent_grad = inv_chan * (
        act_grad * norm_gain
        - jnp.repeat(mean_q, per_group)
        - normed * jnp.repeat(mean_qn, per_group)
    )
    return (latent_grad, gain_grad, bias_grad)


def solution(mesh):
    placed = (
        P("tm", "rows", None, None),
        P(),
        P(),
        P(None, None, None, "rows", "tm"),
        P("tm", "rows", None, None),
    )
    return jax.shard_map(
        on_device,
        mesh=mesh,
        in_specs=placed,
        out_specs=(P("tm", "rows", None, None), P(), P()),
        check_vma=False,
    )
```

profile of v0, /device:TPU:1, one launch (start us, length us, event | category | flops | bytes accessed | tf_op | source)
XLA Modules:
  0.0 354.6 jit_solution(4041163253013684087)
XLA Ops:
  7.2 11.7 %all_gather.6 = bf16[3,3,3,8,512]{4,3,2,1,0:T(8,128)(2,1)} all-gather(bf16[3,3,3,8,128]{4,3,2,1,0:T(8,128)(2,1)} %param.10), channel_id=1, replica_groups=mesh['tm'=4,'rows'=64] {'tm'}, dimensions={4}, use_global_device_ids=true | all-gather | bytes 276480 | tf_op jit(solution)/shard_map/all_gather | solution.py:84
  20.1 6.2 %collective-permute-start = (bf16[1,1,320,512]{3,2,1,0:T(8,128)(2,1)S(1)}, bf16[1,1,320,512]{3,2,1,0:T(8,128)(2,1)S(1)}, u32[]{:S(2)}, u32[]{:S(2)}) collective-permute-start(bf16[1,1,320,512]{3,2,1,0:T(8,128)(2,1)S(1)} %get-tuple-element.27), channel_id=1, source_target_pairs={{0,1},{1,2},{2,3},{3,4},{4,5},{5,6},{6,7},{7,8},{8,9},{9,10},{10,1... | collective-permute-start | bytes 983048 | tf_op jit(solution)/shard_map/ppermute | solution.py:14
  26.3 1.9 collective-permute-start.1
  28.2 2.1 collective-permute-done
  30.4 4.3 %collective-permute-done.1 = bf16[1,1,320,512]{3,2,1,0:T(8,128)(2,1)S(1)} collective-permute-done((bf16[1,1,320,512]{3,2,1,0:T(8,128)(2,1)S(1)}, bf16[1,1,320,512]{3,2,1,0:T(8,128)(2,1)S(1)}, u32[]{:S(2)}, u32[]{:S(2)}) %collective-permute-start.1) | collective-permute-done | bytes 327712 | tf_op jit(solution)/shard_map/ppermute | solution.py:17
  37.6 129.7 %all-reduce.2 = (f32[32,16]{1,0:T(8,128)S(1)}, f32[32,16]{1,0:T(8,128)S(1)}) all-reduce(f32[32,16]{1,0:T(8,128)S(1)} %reshape.178, f32[32,16]{1,0:T(8,128)S(1)} %reshape.177), channel_id=1, replica_groups=mesh['tm'=4,'rows'=64] {'tm','rows'}, use_global_device_ids=true, to_apply=%region_4.5 | all-reduce | flops 1024 | bytes 8192 | tf_op jit(solution)/shard_map/psum | solution.py:90
  167.8 3.9 %fusion.113 = bf16[3,4,322,512]{3,2,1,0:T(8,128)(2,1)} fusion(bf16[1,4,320,512]{3,2,1,0:T(8,128)(2,1)} %collective-permute-done.3, bf16[1,4,320,512]{3,2,1,0:T(8,128)(2,1)} %collective-permute-done.2, bf16[1,4,320,512]{3,2,1,0:T(8,128)(2,1)S(1)} %constant_dynamic-update-slice_fusion), kind=kLoop, calls=%fused_computation.168 | loop fusion | flops 23740416 | bytes 7888896 | tf_op jit(solution)/shard_map/concatenate | solution.py:83
  171.7 48.1 %conditional.1 = (f32[1,2,320,512]{3,2,1,0:T(8,128)}) conditional(s32[]{:T(128)} %convert_element_type.9, () %tuple.14, (bf16[3,4,322,512]{3,2,1,0:T(8,128)(2,1)}, bf16[3,3,3,512,512]{4,3,2,1,0:T(8,128)(2,1)}) %tuple.15), branch_computations={%region_6.7_spmd, %region_7.8_spmd} | conditional | flops 9124839424 | bytes 177053760 | solution.py:68
  171.7 1.9 convolution_bitcast_fusion.15
  173.6 1.8 convolution_bitcast_fusion.16
  175.5 1.7 convolution_bitcast_fusion.17
  177.2 2.0 convolution_bitcast_fusion.24
  179.2 2.1 convolution_bitcast_fusion.25
  189.4 1.6 convolution_bitcast_fusion.19
  191.0 1.6 convolution_bitcast_fusion.6
  192.7 1.6 convolution_bitcast_fusion.7
  194.3 1.7 convolution_bitcast_fusion.3
  195.9 1.6 convolution_bitcast_fusion.4
  197.5 1.6 convolution_bitcast_fusion
  199.2 1.6 convolution_bitcast_fusion.1
  200.8 1.6 convolution_bitcast_fusion.2
  202.4 1.7 convolution_bitcast_fusion.5
  204.1 1.7 convolution_bitcast_fusion.8
  205.8 1.7 convolution_bitcast_fusion.20
  207.5 1.6 convolution_bitcast_fusion.23
  209.1 1.6 convolution_bitcast_fusion.26
  210.7 9.0 %slice_add_fusion = f32[1,2,320,512]{3,2,1,0:T(8,128)} fusion(f32[1,2,322,512]{3,2,1,0:T(8,128)} %convolution_bitcast_fusion, f32[1,2,322,512]{3,2,1,0:T(8,128)} %convolution_bitcast_fusion.1, f32[1,2,322,512]{3,2,1,0:T(8,128)} %convolution_bitcast_fusion.2, f32[1,2,322,512]{3,2,1,0:T(8,128)} %convolution_bitcast_fusion.3, ...), kind=kLoop, calls=%fused_computation.27 | loop fusion | flops 8519680 | bytes 36700160 | tf_op jit(solution)/shard_map/cond/branch_1_fun/add | solution.py:47
  219.8 1.9 convolution_bitcast_fusion.28
  221.7 1.8 convolution_bitcast_fusion.27
  223.6 1.7 convolution_bitcast_fusion.31
  225.3 2.0 convolution_bitcast_fusion.30
  227.3 2.1 convolution_bitcast_fusion.34
  237.0 1.7 convolution_bitcast_fusion.45
  238.7 1.7 convolution_bitcast_fusion.49
  240.4 1.6 convolution_bitcast_fusion.48
  242.0 1.6 convolution_bitcast_fusion.52
  243.6 1.6 convolution_bitcast_fusion.51
  245.2 1.6 convolution_bitcast_fusion.29
  246.9 1.6 convolution_bitcast_fusion.32
  248.5 1.6 convolution_bitcast_fusion.35
  250.1 1.6 convolution_bitcast_fusion.38
  251.7 1.7 convolution_bitcast_fusion.41
  253.4 1.6 convolution_bitcast_fusion.44
  255.0 1.6 convolution_bitcast_fusion.47
  256.6 1.6 convolution_bitcast_fusion.50
  258.2 1.7 convolution_bitcast_fusion.53
  259.9 10.1 %fusion.115 = f32[320,512]{1,0:T(8,128)} fusion(f32[1,2,320,512]{3,2,1,0:T(8,128)} %get-tuple-element.34, f32[1,2,322,512]{3,2,1,0:T(8,128)S(1)} %convolution_bitcast_fusion.27, f32[1,2,322,512]{3,2,1,0:T(8,128)S(1)} %convolution_bitcast_fusion.28, f32[1,2,322,512]{3,2,1,0:T(8,128)} %convolution_bitcast_fusion.29, ...), kind=kLoop, calls=%fused_computation.198 | loop fusion | flops 9011200 | bytes 37355520 | tf_op jit(solution)/shard_map/reduce_sum | solution.py:53
  272.5 73.1 %all-reduce.1 = (f32[512]{0:T(512)S(1)}, f32[512]{0:T(512)S(1)}) all-reduce(f32[512]{0:T(512)S(1)} %get-tuple-element.18, f32[512]{0:T(512)S(1)} %get-tuple-element.17), channel_id=1, replica_groups=mesh['tm'=4,'rows'=64] {'tm','rows'}, use_global_device_ids=true, to_apply=%region_14.15 | all-reduce | flops 1024 | bytes 8192 | tf_op jit(solution)/shard_map/psum | solution.py:102
  (69 shorter events, 24.7 us)
Async XLA Ops:
  7.2 23.2 %copy-start.4 = (bf16[1,2,320,512]{3,2,1,0:T(8,128)(2,1)S(1)}, bf16[1,2,320,512]{3,2,1,0:T(8,128)(2,1)}, u32[]{:S(2)}) copy-start(bf16[1,2,320,512]{3,2,1,0:T(8,128)(2,1)} %param.11) | copy-start | bytes 1966084
  7.2 164.5 %all-gather.2.cloned.1.call-start = ((), (), s32[]{:S(2)}) async-start(), calls=%async_computation | async-start | bytes 14376960 | tf_op jit(solution)/shard_map/all_gather | solution.py:85
  20.0 17.3 %copy-start.5 = (bf16[1,1,160,512]{3,2,1,0:T(8,128)(2,1)S(1)}, bf16[1,1,160,512]{3,2,1,0:T(8,128)(2,1)}, u32[]{:S(2)}) copy-start(bf16[1,1,160,512]{3,2,1,0:T(8,128)(2,1)} %param.7) | copy-start | bytes 491524
  20.1 10.2 %collective-permute-start = (bf16[1,1,320,512]{3,2,1,0:T(8,128)(2,1)S(1)}, bf16[1,1,320,512]{3,2,1,0:T(8,128)(2,1)S(1)}, u32[]{:S(2)}, u32[]{:S(2)}) collective-permute-start(bf16[1,1,320,512]{3,2,1,0:T(8,128)(2,1)S(1)} %get-tuple-element.27), channel_id=1, source_target_pairs={{0,1},{1,2},{2,3},{3,4},{4,5},{5,6},{6,7},{7,8},{8,9},{9,10},{10,1... | collective-permute-start | bytes 983048 | tf_op jit(solution)/shard_map/ppermute | solution.py:14
  26.3 8.4 %collective-permute-start.1 = (bf16[1,1,320,512]{3,2,1,0:T(8,128)(2,1)S(1)}, bf16[1,1,320,512]{3,2,1,0:T(8,128)(2,1)S(1)}, u32[]{:S(2)}, u32[]{:S(2)}) collective-permute-start(bf16[1,1,320,512]{3,2,1,0:T(8,128)(2,1)S(1)} %get-tuple-element.26), channel_id=1, source_target_pairs={{1,0},{2,1},{3,2},{4,3},{5,4},{6,5},{7,6},{8,7},{9,8},{10,9},{11,1... | collective-permute-start | bytes 983048 | tf_op jit(solution)/shard_map/ppermute | solution.py:17
  34.7 133.1 %collective-permute-start.3 = (bf16[1,4,320,512]{3,2,1,0:T(8,128)(2,1)S(1)}, bf16[1,4,320,512]{3,2,1,0:T(8,128)(2,1)}, u32[]{:S(2)}, u32[]{:S(2)}) collective-permute-start(bf16[1,4,320,512]{3,2,1,0:T(8,128)(2,1)S(1)} %constant_dynamic-update-slice_fusion), channel_id=1, source_target_pairs={{128,0},{192,64},{129,1},{193,65},{130,2},{194,66},{131,3},{195,67... | collective-permute-start | bytes 3932168 | tf_op jit(solution)/shard_map/ppermute | solution.py:25
  36.0 131.8 %collective-permute-start.2 = (bf16[1,4,320,512]{3,2,1,0:T(8,128)(2,1)S(1)}, bf16[1,4,320,512]{3,2,1,0:T(8,128)(2,1)}, u32[]{:S(2)}, u32[]{:S(2)}) collective-permute-start(bf16[1,4,320,512]{3,2,1,0:T(8,128)(2,1)S(1)} %constant_dynamic-update-slice_fusion), channel_id=1, source_target_pairs={{64,0},{128,64},{192,128},{65,1},{129,65},{193,129},{66,2},{130,66... | collective-permute-start | bytes 3932168 | tf_op jit(solution)/shard_map/ppermute | solution.py:25
  171.7 3.7 %copy-start.1 = (bf16[3,4,322,512]{3,2,1,0:T(8,128)(2,1)S(1)}, bf16[3,4,322,512]{3,2,1,0:T(8,128)(2,1)}, u32[]{:S(2)}) copy-start(bf16[3,4,322,512]{3,2,1,0:T(8,128)(2,1)} %get-tuple-element.12) | copy-start | bytes 11870212 | tf_op jit(solution)/shard_map/cond
  175.4 10.7 %copy-start.3 = (bf16[3,3,3,512,512]{4,3,2,1,0:T(8,128)(2,1)S(1)}, bf16[3,3,3,512,512]{4,3,2,1,0:T(8,128)(2,1)}, u32[]{:S(2)}) copy-start(bf16[3,3,3,512,512]{4,3,2,1,0:T(8,128)(2,1)} %get-tuple-element.13) | copy-start | bytes 42467332 | tf_op jit(solution)/shard_map/cond
  219.8 3.7 %copy-start = (bf16[3,4,322,512]{3,2,1,0:T(8,128)(2,1)S(1)}, bf16[3,4,322,512]{3,2,1,0:T(8,128)(2,1)}, u32[]{:S(2)}) copy-start(bf16[3,4,322,512]{3,2,1,0:T(8,128)(2,1)} %fusion.113) | copy-start | bytes 11870212
  223.5 10.7 %copy-start.2 = (bf16[3,3,3,512,512]{4,3,2,1,0:T(8,128)(2,1)S(1)}, bf16[3,3,3,512,512]{4,3,2,1,0:T(8,128)(2,1)}, u32[]{:S(2)}) copy-start(bf16[3,3,3,512,512]{4,3,2,1,0:T(8,128)(2,1)} %all-gather.2.cloned.1.call-done) | copy-start | bytes 42467332
  270.0 2.3 copy-start.6
  270.0 2.3 copy-start.7
Sparse Core Ops, SparseCore 0:
  19.0 105.3 all-gather.1
where the time goes:
time: 355 us
  blocking collectives  214 us (60%)
  matrix products  78.8 us (22%)
  other arithmetic  26 us (7%)
  between operations  14.3 us (4%)
  starting transfers between devices  10.8 us (3%)
  waiting for transfers between devices  6.41 us (2%)
  local copies, waits for them, and re-layouts  3.66 us (1%)
    psum x1, blocking collectives, on_device(): total_x, total_sq = lax.psum((sum_x, sum_sq), ('tm', 'rows'))  130 us
    dot_general x54, matrix products, tap_total(): lax.dot_general(source, weights[tap_index, row_tap, col_tap], (((3,), (1,...  78.8 us
    psum x1, blocking collectives, on_device(): lax.psum((jnp.sum(act_grad, axis=(0, 1, 2)), jnp.sum(act_grad * normed, a...  73.1 us
    all_gather x1, blocking collectives, on_device(): weight_wide = lax.all_gather(conv_weight, 'tm', axis=4, tiled=True)  11.7 us
    reduce_sum x2, other arithmetic, pool_pairs(): fine_grad.reshape(frames, fine_rows // 2, 2, span_cols // 2, 2, channels)  10.9 us
    add x1, other arithmetic, tap_total(): running = piece if running is None else running + piece  9.05 us
  transfers between devices with their start and end apart: 5, of which 2 were waited for; matrix products, arithmetic and copies ran while one was open for 2% of the time, Pallas kernels for 0%

commit v1 on v0

--- a/solution.py
+++ b/solution.py
@@ -87,7 +87,7 @@
     features = latent.astype(jnp.float32)
     sum_x = jnp.sum(features, axis=(0, 1, 2))
     sum_sq = jnp.sum(features * features, axis=(0, 1, 2))
-    total_x, total_sq = lax.psum((sum_x, sum_sq), ("tm", "rows"))
+    total_x, total_sq = lax.psum(lax.psum((sum_x, sum_sq), "rows"), "tm")
     group_x = total_x.reshape(GROUPS, per_group).sum(axis=1)
     group_sq = total_sq.reshape(GROUPS, per_group).sum(axis=1)
     group_mean = group_x / (cell_count * per_group)

time: 355 us -> 372 us (1.048)
  blocking collectives: 214 us -> 231 us
    psum x1 -> x2, blocking collectives: 130 us -> 144 us  [on_device(): total_x, total_sq = lax.psum(lax.psum((sum_x, sum_sq), 'rows'), 'tm')]
where the time goes in v1:
time: 372 us; the launch traced here: 371 us
  blocking collectives  231 us (62%)
  matrix products  78.8 us (21%)
  other arithmetic  26 us (7%)
  between operations  14.3 us (4%)
  starting transfers between devices  10.8 us (3%)
  waiting for transfers between devices  6.41 us (2%)
    psum x2, blocking collectives, on_device(): total_x, total_sq = lax.psum(lax.psum((sum_x, sum_sq), 'rows'), 'tm')  144 us
    dot_general x54, matrix products, tap_total(): lax.dot_general(source, weights[tap_index, row_tap, col_tap], (((3,), (1,...  78.8 us
    psum x1, blocking collectives, on_device(): lax.psum((jnp.sum(act_grad, axis=(0, 1, 2)), jnp.sum(act_grad * normed, a...  75.8 us
    all_gather x1, blocking collectives, on_device(): weight_wide = lax.all_gather(conv_weight, 'tm', axis=4, tiled=True)  11.7 us
    reduce_sum x2, other arithmetic, pool_pairs(): fine_grad.reshape(frames, fine_rows // 2, 2, span_cols // 2, 2, channels)  10.9 us
    add x1, other arithmetic, tap_total(): running = piece if running is None else running + piece  9.05 us
  transfers between devices with their start and end apart: 5, of which 2 were waited for; matrix products, arithmetic and copies ran while one was open for 2% of the time, Pallas kernels for 0%

profile of v1, /device:TPU:1, one launch (start us, length us, event | category | flops | bytes accessed | tf_op | source)
XLA Modules:
  0.0 371.4 jit_solution(4181353721721706872)
XLA Ops:
  7.2 11.7 %all_gather.6 = bf16[3,3,3,8,512]{4,3,2,1,0:T(8,128)(2,1)} all-gather(bf16[3,3,3,8,128]{4,3,2,1,0:T(8,128)(2,1)} %param.10), channel_id=1, replica_groups=mesh['tm'=4,'rows'=64] {'tm'}, dimensions={4}, use_global_device_ids=true | all-gather | bytes 276480 | tf_op jit(solution)/shard_map/all_gather | solution.py:84
  20.1 6.2 %collective-permute-start = (bf16[1,1,320,512]{3,2,1,0:T(8,128)(2,1)S(1)}, bf16[1,1,320,512]{3,2,1,0:T(8,128)(2,1)S(1)}, u32[]{:S(2)}, u32[]{:S(2)}) collective-permute-start(bf16[1,1,320,512]{3,2,1,0:T(8,128)(2,1)S(1)} %get-tuple-element.29), channel_id=1, source_target_pairs={{0,1},{1,2},{2,3},{3,4},{4,5},{5,6},{6,7},{7,8},{8,9},{9,10},{10,1... | collective-permute-start | bytes 983048 | tf_op jit(solution)/shard_map/ppermute | solution.py:14
  26.3 1.9 collective-permute-start.1
  28.2 2.1 collective-permute-done
  30.4 4.3 %collective-permute-done.1 = bf16[1,1,320,512]{3,2,1,0:T(8,128)(2,1)S(1)} collective-permute-done((bf16[1,1,320,512]{3,2,1,0:T(8,128)(2,1)S(1)}, bf16[1,1,320,512]{3,2,1,0:T(8,128)(2,1)S(1)}, u32[]{:S(2)}, u32[]{:S(2)}) %collective-permute-start.1) | collective-permute-done | bytes 327712 | tf_op jit(solution)/shard_map/ppermute | solution.py:17
  37.4 125.8 %all-reduce.2 = (f32[512]{0:T(512)S(1)}, f32[512]{0:T(512)S(1)}) all-reduce(f32[512]{0:T(512)S(1)} %get-tuple-element.20, f32[512]{0:T(512)S(1)} %get-tuple-element.19), channel_id=1, replica_groups=mesh['tm'=4,'rows'=64] {'rows'}, use_global_device_ids=true, to_apply=%region_5.6 | all-reduce | flops 1024 | bytes 8192 | tf_op jit(solution)/shard_map/psum | solution.py:90
  163.4 17.9 %all-reduce.3 = (f32[32,16]{1,0:T(8,128)S(1)}, f32[32,16]{1,0:T(8,128)S(1)}) all-reduce(f32[32,16]{1,0:T(8,128)S(1)} %reshape.178, f32[32,16]{1,0:T(8,128)S(1)} %reshape.177), channel_id=1, replica_groups=mesh['tm'=4,'rows'=64] {'tm'}, use_global_device_ids=true, to_apply=%region_6.7 | all-reduce | flops 1024 | bytes 8192 | tf_op jit(solution)/shard_map/psum | solution.py:90
  181.9 3.9 %fusion.113 = bf16[3,4,322,512]{3,2,1,0:T(8,128)(2,1)} fusion(bf16[1,4,320,512]{3,2,1,0:T(8,128)(2,1)} %collective-permute-done.3, bf16[1,4,320,512]{3,2,1,0:T(8,128)(2,1)} %collective-permute-done.2, bf16[1,4,320,512]{3,2,1,0:T(8,128)(2,1)S(1)} %constant_dynamic-update-slice_fusion), kind=kLoop, calls=%fused_computation.168 | loop fusion | flops 23740416 | bytes 7888896 | tf_op jit(solution)/shard_map/concatenate | solution.py:83
  185.8 48.1 %conditional.1 = (f32[1,2,320,512]{3,2,1,0:T(8,128)}) conditional(s32[]{:T(128)} %convert_element_type.9, () %tuple.14, (bf16[3,4,322,512]{3,2,1,0:T(8,128)(2,1)}, bf16[3,3,3,512,512]{4,3,2,1,0:T(8,128)(2,1)}) %tuple.15), branch_computations={%region_8.9_spmd, %region_9.10_spmd} | conditional | flops 9124839424 | bytes 177053760 | solution.py:68
  185.8 1.9 convolution_bitcast_fusion.15
  187.7 1.8 convolution_bitcast_fusion.16
  189.5 1.7 convolution_bitcast_fusion.17
  191.3 2.0 convolution_bitcast_fusion.24
  193.3 2.1 convolution_bitcast_fusion.25
  203.5 1.6 convolution_bitcast_fusion.19
  205.1 1.6 convolution_bitcast_fusion.6
  206.8 1.6 convolution_bitcast_fusion.7
  208.4 1.7 convolution_bitcast_fusion.3
  210.0 1.6 convolution_bitcast_fusion.4
  211.6 1.6 convolution_bitcast_fusion
  213.3 1.6 convolution_bitcast_fusion.1
  216.5 1.7 convolution_bitcast_fusion.5
  218.2 1.7 convolution_bitcast_fusion.8
  219.9 1.7 convolution_bitcast_fusion.20
  221.5 1.6 convolution_bitcast_fusion.23
  223.2 1.6 convolution_bitcast_fusion.26
  224.8 9.0 %slice_add_fusion = f32[1,2,320,512]{3,2,1,0:T(8,128)} fusion(f32[1,2,322,512]{3,2,1,0:T(8,128)} %convolution_bitcast_fusion, f32[1,2,322,512]{3,2,1,0:T(8,128)} %convolution_bitcast_fusion.1, f32[1,2,322,512]{3,2,1,0:T(8,128)} %convolution_bitcast_fusion.2, f32[1,2,322,512]{3,2,1,0:T(8,128)} %convolution_bitcast_fusion.3, ...), kind=kLoop, calls=%fused_computation.27 | loop fusion | flops 8519680 | bytes 36700160 | tf_op jit(solution)/shard_map/cond/branch_1_fun/add | solution.py:47
  233.9 1.9 convolution_bitcast_fusion.28
  235.8 1.8 convolution_bitcast_fusion.27
  237.6 1.7 convolution_bitcast_fusion.31
  239.4 2.0 convolution_bitcast_fusion.30
  241.4 2.1 convolution_bitcast_fusion.34
  251.1 1.7 convolution_bitcast_fusion.45
  252.8 1.7 convolution_bitcast_fusion.49
  254.5 1.6 convolution_bitcast_fusion.48
  256.1 1.6 convolution_bitcast_fusion.52
  257.7 1.6 convolution_bitcast_fusion.51
  259.3 1.6 convolution_bitcast_fusion.29
  261.0 1.6 convolution_bitcast_fusion.32
  262.6 1.6 convolution_bitcast_fusion.35
  264.2 1.6 convolution_bitcast_fusion.38
  265.8 1.7 convolution_bitcast_fusion.41
  267.5 1.6 convolution_bitcast_fusion.44
  269.1 1.6 convolution_bitcast_fusion.47
  270.7 1.6 convolution_bitcast_fusion.50
  272.3 1.7 convolution_bitcast_fusion.53
  274.0 10.1 %fusion.115 = f32[320,512]{1,0:T(8,128)} fusion(f32[1,2,320,512]{3,2,1,0:T(8,128)} %get-tuple-element.36, f32[1,2,322,512]{3,2,1,0:T(8,128)S(1)} %convolution_bitcast_fusion.27, f32[1,2,322,512]{3,2,1,0:T(8,128)S(1)} %convolution_bitcast_fusion.28, f32[1,2,322,512]{3,2,1,0:T(8,128)} %convolution_bitcast_fusion.29, ...), kind=kLoop, calls=%fused_computation.198 | loop fusion | flops 9011200 | bytes 37355520 | tf_op jit(solution)/shard_map/reduce_sum | solution.py:53
  286.6 75.8 %all-reduce.1 = (f32[512]{0:T(512)S(1)}, f32[512]{0:T(512)S(1)}) all-reduce(f32[512]{0:T(512)S(1)} %get-tuple-element.18, f32[512]{0:T(512)S(1)} %get-tuple-element.17), channel_id=1, replica_groups=mesh['tm'=4,'rows'=64] {'tm','rows'}, use_global_device_ids=true, to_apply=%region_16.17 | all-reduce | flops 1024 | bytes 8192 | tf_op jit(solution)/shard_map/psum | solution.py:102
  (70 shorter events, 26.3 us)
Async XLA Ops:
  7.2 23.2 %copy-start.4 = (bf16[1,2,320,512]{3,2,1,0:T(8,128)(2,1)S(1)}, bf16[1,2,320,512]{3,2,1,0:T(8,128)(2,1)}, u32[]{:S(2)}) copy-start(bf16[1,2,320,512]{3,2,1,0:T(8,128)(2,1)} %param.11) | copy-start | bytes 1966084
  7.2 178.6 %all-gather.2.cloned.1.call-start = ((), (), s32[]{:S(2)}) async-start(), calls=%async_computation | async-start | bytes 14376960 | tf_op jit(solution)/shard_map/all_gather | solution.py:85
  20.0 17.3 %copy-start.5 = (bf16[1,1,160,512]{3,2,1,0:T(8,128)(2,1)S(1)}, bf16[1,1,160,512]{3,2,1,0:T(8,128)(2,1)}, u32[]{:S(2)}) copy-start(bf16[1,1,160,512]{3,2,1,0:T(8,128)(2,1)} %param.7) | copy-start | bytes 491524
  20.1 10.2 %collective-permute-start = (bf16[1,1,320,512]{3,2,1,0:T(8,128)(2,1)S(1)}, bf16[1,1,320,512]{3,2,1,0:T(8,128)(2,1)S(1)}, u32[]{:S(2)}, u32[]{:S(2)}) collective-permute-start(bf16[1,1,320,512]{3,2,1,0:T(8,128)(2,1)S(1)} %get-tuple-element.29), channel_id=1, source_target_pairs={{0,1},{1,2},{2,3},{3,4},{4,5},{5,6},{6,7},{7,8},{8,9},{9,10},{10,1... | collective-permute-start | bytes 983048 | tf_op jit(solution)/shard_map/ppermute | solution.py:14
  26.3 8.4 %collective-permute-start.1 = (bf16[1,1,320,512]{3,2,1,0:T(8,128)(2,1)S(1)}, bf16[1,1,320,512]{3,2,1,0:T(8,128)(2,1)S(1)}, u32[]{:S(2)}, u32[]{:S(2)}) collective-permute-start(bf16[1,1,320,512]{3,2,1,0:T(8,128)(2,1)S(1)} %get-tuple-element.28), channel_id=1, source_target_pairs={{1,0},{2,1},{3,2},{4,3},{5,4},{6,5},{7,6},{8,7},{9,8},{10,9},{11,1... | collective-permute-start | bytes 983048 | tf_op jit(solution)/shard_map/ppermute | solution.py:17
  34.7 147.2 %collective-permute-start.3 = (bf16[1,4,320,512]{3,2,1,0:T(8,128)(2,1)S(1)}, bf16[1,4,320,512]{3,2,1,0:T(8,128)(2,1)}, u32[]{:S(2)}, u32[]{:S(2)}) collective-permute-start(bf16[1,4,320,512]{3,2,1,0:T(8,128)(2,1)S(1)} %constant_dynamic-update-slice_fusion), channel_id=1, source_target_pairs={{128,0},{192,64},{129,1},{193,65},{130,2},{194,66},{131,3},{195,67... | collective-permute-start | bytes 3932168 | tf_op jit(solution)/shard_map/ppermute | solution.py:25
  36.0 145.9 %collective-permute-start.2 = (bf16[1,4,320,512]{3,2,1,0:T(8,128)(2,1)S(1)}, bf16[1,4,320,512]{3,2,1,0:T(8,128)(2,1)}, u32[]{:S(2)}, u32[]{:S(2)}) collective-permute-start(bf16[1,4,320,512]{3,2,1,0:T(8,128)(2,1)S(1)} %constant_dynamic-update-slice_fusion), channel_id=1, source_target_pairs={{64,0},{128,64},{192,128},{65,1},{129,65},{193,129},{66,2},{130,66... | collective-permute-start | bytes 3932168 | tf_op jit(solution)/shard_map/ppermute | solution.py:25
  185.8 3.7 %copy-start.1 = (bf16[3,4,322,512]{3,2,1,0:T(8,128)(2,1)S(1)}, bf16[3,4,322,512]{3,2,1,0:T(8,128)(2,1)}, u32[]{:S(2)}) copy-start(bf16[3,4,322,512]{3,2,1,0:T(8,128)(2,1)} %get-tuple-element.12) | copy-start | bytes 11870212 | tf_op jit(solution)/shard_map/cond
  189.5 10.7 %copy-start.3 = (bf16[3,3,3,512,512]{4,3,2,1,0:T(8,128)(2,1)S(1)}, bf16[3,3,3,512,512]{4,3,2,1,0:T(8,128)(2,1)}, u32[]{:S(2)}) copy-start(bf16[3,3,3,512,512]{4,3,2,1,0:T(8,128)(2,1)} %get-tuple-element.13) | copy-start | bytes 42467332 | tf_op jit(solution)/shard_map/cond
  233.9 3.7 %copy-start = (bf16[3,4,322,512]{3,2,1,0:T(8,128)(2,1)S(1)}, bf16[3,4,322,512]{3,2,1,0:T(8,128)(2,1)}, u32[]{:S(2)}) copy-start(bf16[3,4,322,512]{3,2,1,0:T(8,128)(2,1)} %fusion.113) | copy-start | bytes 11870212
  237.6 10.7 %copy-start.2 = (bf16[3,3,3,512,512]{4,3,2,1,0:T(8,128)(2,1)S(1)}, bf16[3,3,3,512,512]{4,3,2,1,0:T(8,128)(2,1)}, u32[]{:S(2)}) copy-start(bf16[3,3,3,512,512]{4,3,2,1,0:T(8,128)(2,1)} %all-gather.2.cloned.1.call-done) | copy-start | bytes 42467332
  284.1 2.3 copy-start.6
  284.1 2.3 copy-start.7
Sparse Core Ops, SparseCore 0:
  19.0 105.6 all-gather.1
